TPU v7x, 128 devices: a whole 4x4x4 slice. The times are simulated.
128 devices in a mesh: dp: 32 (over x, y, core), tensor: 4 (over z).
Axes of the slice: x: 4, y: 4, z: 4, core: 2. Of those that a mesh axis runs over, the one named last changes fastest.
Arguments:
- activations: bfloat16 [65536, 8192], P('dp', 'tensor'), may hold values from -16 to 16
- whitening: bfloat16 [8192, 1024], P('tensor'), may hold values from -8 to 8
- factor: bfloat16 [1024, 1024], P(('dp', 'tensor')), may hold values from -2 to 2
Outputs:
- new_factor: float32 [1024, 1024], P(('dp', 'tensor'))
All inputs are finite; a program needn't handle non-finite values.
Results may differ from a plain program's by a relative error of at most 0.029.
Values may be sent and summed in bfloat16 or wider, within the bound.
A program may use at most 192 MiB of HBM per device.

v0:
```python
import jax
import jax.numpy as jnp
from jax import lax
from jax.sharding import PartitionSpec as P

ridge_shift = 0.1
epsilon = 1e-06


def solve_rows(moment_rows, hadamard):
    lower = jnp.linalg.cholesky(hadamard)
    first = jax.scipy.linalg.solve_triangular(lower, moment_rows.T, lower=True)
    second = jax.scipy.linalg.solve_triangular(lower, first, lower=True, trans=1)
    return second.T


def shards(activations, whitening, factor):
    summed = lax.psum_scatter(
        jnp.dot(activations, whitening, preferred_element_type=jnp.float32).astype(jnp.bfloat16),
        "tensor",
        scatter_dimension=0,
        tiled=True,
    )
    whole_factor = lax.all_gather(factor, ("dp", "tensor"), axis=0, tiled=True)
    projected = jnp.dot(summed, whole_factor, preferred_element_type=jnp.float32)
    squared = (projected * projected).astype(jnp.bfloat16)
    moment_rows = lax.psum_scatter(
        lax.dot_general(
            summed, squared, (((0,), (0,)), ((), ())), preferred_element_type=jnp.float32
        ),
        ("dp", "tensor"),
        scatter_dimension=0,
        tiled=True,
    )
    gram = jnp.dot(whole_factor.T, whole_factor, preferred_element_type=jnp.float32)
    hadamard = gram * gram + ridge_shift * jnp.eye(gram.shape[0], dtype=jnp.float32)
    updated = solve_rows(moment_rows, hadamard)
    column_total = lax.psum(jnp.sum(updated * updated, axis=0), ("dp", "tensor"))
    scale = jnp.sqrt(column_total / whole_factor.shape[0] + epsilon)
    return updated / scale[None, :]


def solution(mesh):
    placed = (P("dp", "tensor"), P("tensor", None), P(("dp", "tensor"), None))
    return jax.shard_map(
        shards, mesh=mesh, in_specs=placed, out_specs=P(("dp", "tensor"), None), check_vma=False
    )
```

profile of v0, /device:TPU:1, one launch (start us, length us, event | category | flops | bytes accessed | tf_op | source)
XLA Modules:
  0.0 901.7 jit_solution(2923321162316526728)
XLA Ops:
  8.1 13.8 %convolution_convert_fusion = bf16[2048,1024]{1,0:T(8,128)(2,1)} fusion(bf16[2048,2048]{1,0:T(8,128)(2,1)} %param.3, bf16[2048,1024]{1,0:T(8,128)(2,1)} %param.4), kind=kOutput, calls=%fused_computation.8 | convolution fusion | flops 8592031744 | bytes 16777216 | tf_op jit(solution)/shard_map/dot_general | solution.py:19
  22.0 77.6 %all-gather.2.cloned.1.call-done = bf16[1024,1024]{1,0:T(8,128)(2,1)} async-done(((bf16[8,1024]{1,0:T(8,128)(2,1)}), bf16[1024,1024]{1,0:T(8,128)(2,1)}) %all-gather.2.cloned.1.call-update) | async-done | bytes 2097168 | tf_op jit(solution)/shard_map/all_gather | solution.py:24
  99.6 4.6 fusion.95
  104.3 2.0 copy-done
  106.2 2.4 multiply_bitcast_fusion
  108.6 5.8 copy.4
  114.4 4.5 add_multiply_fusion
  118.9 2.0 copy-done.1
  120.9 11.7 %cholesky.222 = f32[128,128]{1,0:T(8,128)S(1)} custom-call(f32[128,128]{1,0:T(8,128)S(1)} %cholesky.577), custom_call_target="Cholesky" | custom-call | tf_op jit(solution)/shard_map/jit(cholesky)/cholesky | solution.py:11
  132.6 2.5 cholesky.254
  135.1 9.8 %custom-call.66 = f32[1,128,128]{1,2,0:T(8,128)S(1)} custom-call(f32[1,128,128]{2,1,0:T(8,128)S(1)} %get-tuple-element.44), custom_call_target="InvertDiagBlocksLowerTriangular" | custom-call | tf_op jit(solution)/shard_map/jit(cholesky)/cholesky | solution.py:11
  144.9 2.3 constant_dynamic-update-slice_fusion.50
  147.3 1.5 convolution_subtract_fusion
  148.8 11.8 %cholesky.243 = f32[128,128]{1,0:T(8,128)S(1)} custom-call(f32[128,128]{1,0:T(8,128)S(1)} %cholesky.581), custom_call_target="Cholesky" | custom-call | tf_op jit(solution)/shard_map/jit(cholesky)/cholesky | solution.py:11
  160.7 5.9 fusion.1
  167.3 9.8 %custom-call.67 = f32[1,128,128]{1,2,0:T(8,128)S(1)} custom-call(f32[1,128,128]{2,1,0:T(8,128)S(1)} %get-tuple-element.41), custom_call_target="InvertDiagBlocksLowerTriangular" | custom-call | tf_op jit(solution)/shard_map/jit(cholesky)/cholesky | solution.py:11
  177.1 1.2 convolution_dynamic-update-slice_fusion
  178.3 2.1 convolution_subtract_fusion.1
  180.4 11.7 %cholesky.466 = f32[128,128]{1,0:T(8,128)S(1)} custom-call(f32[128,128]{1,0:T(8,128)S(1)} %cholesky.586), custom_call_target="Cholesky" | custom-call | tf_op jit(solution)/shard_map/jit(cholesky)/cholesky | solution.py:11
  192.8 9.8 %custom-call.68 = f32[1,128,128]{1,2,0:T(8,128)S(1)} custom-call(f32[1,128,128]{2,1,0:T(8,128)S(1)} %get-tuple-element.38), custom_call_target="InvertDiagBlocksLowerTriangular" | custom-call | tf_op jit(solution)/shard_map/jit(cholesky)/cholesky | solution.py:11
  202.6 1.2 convolution_dynamic-update-slice_fusion.1
  203.8 2.5 convolution_subtract_fusion.2
  206.3 11.7 %cholesky.485 = f32[128,128]{1,0:T(8,128)S(1)} custom-call(f32[128,128]{1,0:T(8,128)S(1)} %cholesky.591), custom_call_target="Cholesky" | custom-call | tf_op jit(solution)/shard_map/jit(cholesky)/cholesky | solution.py:11
  218.7 9.8 %custom-call.69 = f32[1,128,128]{1,2,0:T(8,128)S(1)} custom-call(f32[1,128,128]{2,1,0:T(8,128)S(1)} %get-tuple-element.35), custom_call_target="InvertDiagBlocksLowerTriangular" | custom-call | tf_op jit(solution)/shard_map/jit(cholesky)/cholesky | solution.py:11
  228.5 1.1 convolution_dynamic-update-slice_fusion.2
  229.6 2.4 convolution_subtract_fusion.3
  232.0 11.7 %cholesky.504 = f32[128,128]{1,0:T(8,128)S(1)} custom-call(f32[128,128]{1,0:T(8,128)S(1)} %cholesky.596), custom_call_target="Cholesky" | custom-call | tf_op jit(solution)/shard_map/jit(cholesky)/cholesky | solution.py:11
  244.4 10.2 %custom-call.70 = f32[1,128,128]{1,2,0:T(8,128)S(1)} custom-call(f32[1,128,128]{2,1,0:T(8,128)S(1)} %get-tuple-element.32), custom_call_target="InvertDiagBlocksLowerTriangular" | custom-call | tf_op jit(solution)/shard_map/jit(cholesky)/cholesky | solution.py:11
  254.6 1.0 convolution_dynamic-update-slice_fusion.3
  255.6 2.3 convolution_subtract_fusion.4
  257.9 11.7 %cholesky.524 = f32[128,128]{1,0:T(8,128)S(1)} custom-call(f32[128,128]{1,0:T(8,128)S(1)} %cholesky.601), custom_call_target="Cholesky" | custom-call | tf_op jit(solution)/shard_map/jit(cholesky)/cholesky | solution.py:11
  270.2 9.8 %custom-call.71 = f32[1,128,128]{1,2,0:T(8,128)S(1)} custom-call(f32[1,128,128]{2,1,0:T(8,128)S(1)} %get-tuple-element.29), custom_call_target="InvertDiagBlocksLowerTriangular" | custom-call | tf_op jit(solution)/shard_map/jit(cholesky)/cholesky | solution.py:11
  281.0 2.0 convolution_subtract_fusion.5
  283.0 11.9 %cholesky.544 = f32[128,128]{1,0:T(8,128)S(1)} custom-call(f32[128,128]{1,0:T(8,128)S(1)} %cholesky.606), custom_call_target="Cholesky" | custom-call | tf_op jit(solution)/shard_map/jit(cholesky)/cholesky | solution.py:11
  295.5 9.8 %custom-call.72 = f32[1,128,128]{1,2,0:T(8,128)S(1)} custom-call(f32[1,128,128]{2,1,0:T(8,128)S(1)} %get-tuple-element.26), custom_call_target="InvertDiagBlocksLowerTriangular" | custom-call | tf_op jit(solution)/shard_map/jit(cholesky)/cholesky | solution.py:11
  306.2 1.8 convolution_subtract_fusion.6
  308.0 11.7 %cholesky.562 = f32[128,128]{1,0:T(8,128)S(1)} custom-call(f32[128,128]{1,0:T(8,128)S(1)} %convolution_subtract_fusion.6), custom_call_target="Cholesky" | custom-call | tf_op jit(solution)/shard_map/jit(cholesky)/cholesky | solution.py:11
  329.9 4.8 select_select_fusion
  334.7 22.5 %while.1 = (s32[]{:T(128)}, f32[1024,1024]{1,0:T(8,128)}, s32[8,2]{0,1:T(2,128)S(1)}, f32[8,128,128]{2,1,0:T(8,128)S(1)}, s32[]{:T(128)}) while((s32[]{:T(128)}, f32[1024,1024]{1,0:T(8,128)}, s32[8,2]{0,1:T(2,128)S(1)}, f32[8,128,128]{2,1,0:T(8,128)S(1)}, s32[]{:T(128)}) %tuple.56), condition=%wide.while_cond, body=%wide.while_body.sunk | while | flops 2 | bytes 131189 | solution.py:13
  335.3 2.2 bitcast_dynamic-update-slice_fusion.2
  338.1 2.2 bitcast_dynamic-update-slice_fusion.2
  340.9 2.2 bitcast_dynamic-update-slice_fusion.2
  343.8 2.2 bitcast_dynamic-update-slice_fusion.2
  346.6 2.2 bitcast_dynamic-update-slice_fusion.2
  349.4 2.2 bitcast_dynamic-update-slice_fusion.2
  352.2 2.2 bitcast_dynamic-update-slice_fusion.2
  355.0 2.1 bitcast_dynamic-update-slice_fusion.2
  357.2 78.8 %custom-call.73 = f32[8,128,128]{1,2,0:T(8,128)S(1)} custom-call(f32[8,128,128]{2,1,0:T(8,128)S(1)} %get-tuple-element.12), custom_call_target="InvertDiagBlocksLowerTriangular" | custom-call | tf_op jit(solution)/shard_map/jit(_solve_triangular)/triangular_solve | solution.py:13
  436.0 365.3 %reduce-scatter.5.cloned.1.call-done = f32[8,1024]{1,0:T(8,128)} async-done(((f32[1024,1024]{1,0:T(8,128)}), f32[8,1024]{1,0:T(8,128)}) %reduce-scatter.5.cloned.1.call-update) | async-done | bytes 32784 | tf_op jit(solution)/shard_map/reduce_scatter | solution.py:27
  802.1 1.0 convolution_subtract_fusion.16
  803.3 1.1 convolution_subtract_fusion.15
  804.6 1.2 convolution_subtract_fusion.14
  806.0 1.2 convolution_subtract_fusion.13
  807.5 1.4 convolution_subtract_fusion.12
  809.1 1.4 convolution_subtract_fusion.20
  810.6 1.5 convolution_subtract_fusion.19
  812.7 1.0 convolution_subtract_fusion.11
  814.0 1.1 convolution_subtract_fusion.10
  815.3 1.2 convolution_subtract_fusion.9
  816.7 1.2 convolution_subtract_fusion.8
  818.2 1.3 convolution_subtract_fusion.7
  819.7 1.3 convolution_subtract_fusion.18
  821.3 1.4 convolution_subtract_fusion.17
  823.0 70.4 %psum.7 = f32[1024]{0:T(1024)S(1)} all-reduce(f32[1024]{0:T(1024)S(1)} %multiply_reduce_fusion), channel_id=1, replica_groups=mesh['dp'=32,'tensor'=4] {'dp','tensor'}, use_global_device_ids=true, to_apply=%region_19.20 | all-reduce | flops 1024 | bytes 8192 | tf_op jit(solution)/shard_map/psum | solution.py:38
  (95 shorter events, 21.3 us)
Async XLA Ops:
  7.4 92.3 %all-gather.2.cloned.1.call-start = ((), (), s32[]{:S(2)}) async-start(), calls=%async_computation.2 | async-start | bytes 2113536 | tf_op jit(solution)/shard_map/all_gather | solution.py:24
  8.1 152.6 %reduce-scatter.3.cloned.1.call-start = ((), (), s32[]{:S(2)}) async-start(), calls=%async_computation.3 | async-start | bytes 5242880 | tf_op jit(solution)/shard_map/reduce_scatter | solution.py:18
  21.9 779.3 %reduce-scatter.5.cloned.1.call-start = ((), (), s32[]{:S(2)}) async-start(), calls=%async_computation.4 | async-start | bytes 4227072 | tf_op jit(solution)/shard_map/reduce_scatter | solution.py:27
  104.2 2.0 copy-start
  118.9 2.0 copy-start.1
  120.8 39.9 %copy-start.2 = (bf16[1024,1024]{1,0:T(8,128)(2,1)S(1)}, bf16[1024,1024]{1,0:T(8,128)(2,1)}, u32[]{:S(2)}) copy-start(bf16[1024,1024]{1,0:T(8,128)(2,1)} %all-gather.2.cloned.1.call-done) | copy-start | bytes 6291460
Sparse Core Ops, SparseCore 0:
  11.2 88.4 all-gather.1
  166.7 634.4 reduce-scatter.4
Sparse Core Ops, SparseCore 1:
  22.0 50.3 reduce-scatter.2
where the time goes:
time: 908 us; the launch traced here: 902 us
  waiting for transfers between devices  444 us (49%)
  other arithmetic  263 us (29%)
  blocking collectives  70.4 us (8%)
  matrix products  68.9 us (8%)
  local copies, waits for them, and re-layouts  34.8 us (4%)
  between operations  20.4 us (2%)
    reduce_scatter x1, waiting for transfers between devices, shards(): lax.psum_scatter(lax.dot_general(summed, squared, (((0,), (0,)), ((), ())...  365 us
    another operation x30, other arithmetic, solve_rows(): lower = jnp.linalg.cholesky(hadamard)  172 us
    another operation x3, other arithmetic, solve_rows(): jax.scipy.linalg.solve_triangular(lower, first, lower=True, trans=1)  83.6 us
    all_gather x1, waiting for transfers between devices, shards(): whole_factor = lax.all_gather(factor, ('dp', 'tensor'), axis=0, tiled=True)  77.6 us
    psum x1, blocking collectives, shards(): lax.psum(jnp.sum(updated * updated, axis=0), ('dp', 'tensor'))  70.4 us
    another operation x14, matrix products, solve_rows(): lower = jnp.linalg.cholesky(hadamard)  23.3 us
    another operation x24, local copies, waits for them, and re-layouts  22.3 us
  transfers between devices with their start and end apart: 3, of which 2 were waited for; matrix products, arithmetic and copies ran while one was open for 37% of the time, Pallas kernels for 0%

commit v1 on v0

--- a/solution.py
+++ b/solution.py
@@ -21,7 +21,9 @@
         scatter_dimension=0,
         tiled=True,
     )
-    whole_factor = lax.all_gather(factor, ("dp", "tensor"), axis=0, tiled=True)
+    b_now = jnp.stack([factor for _ in range(lax.axis_size(("dp", "tensor")))])
+    a_next = lax.all_to_all(b_now, ("dp", "tensor"), concat_axis=0, split_axis=0)
+    whole_factor = jnp.concatenate(a_next, 0)
     projected = jnp.dot(summed, whole_factor, preferred_element_type=jnp.float32)
     squared = (projected * projected).astype(jnp.bfloat16)
     moment_rows = lax.psum_scatter(

time: 908 us -> 854 us (0.941)
  waiting for transfers between devices: 444 us -> 379 us
  starting transfers between devices: 0.09 us -> 11.6 us
    all_gather x1 -> x0, waiting for transfers between devices: 77.6 us -> none  [shards(): whole_factor = lax.all_gather(factor, ('dp', 'tensor'), axis=0, tiled=True)]
    all_to_all x0 -> x1, waiting for transfers between devices: none -> 17 us  [shards(): lax.all_to_all(b_now, ('dp', 'tensor'), concat_axis=0, split_axis=0)]
    all_to_all x0 -> x1, starting transfers between devices: none -> 11.5 us  [shards(): lax.all_to_all(b_now, ('dp', 'tensor'), concat_axis=0, split_axis=0)]
    another operation x24 -> x25, local copies, waits for them, and re-layouts: 22.3 us -> 24.6 us
  transfers between devices with their start and end apart: 3 -> 3, of which waited for: 2 -> 2; matrix products, arithmetic and copies ran while one was open for 37% -> 39% of each run, Pallas kernels for 0% -> 0%
where the time goes in v1:
time: 854 us; the launch traced here: 847 us
  waiting for transfers between devices  379 us (44%)
  other arithmetic  263 us (31%)
  blocking collectives  70.4 us (8%)
  matrix products  66.6 us (8%)
  local copies, waits for them, and re-layouts  37.2 us (4%)
  between operations  19 us (2%)
  starting transfers between devices  11.6 us (1%)
    reduce_scatter x1, waiting for transfers between devices, shards(): lax.psum_scatter(lax.dot_general(summed, squared, (((0,), (0,)), ((), ())...  362 us
    another operation x30, other arithmetic, solve_rows(): lower = jnp.linalg.cholesky(hadamard)  172 us
    another operation x3, other arithmetic, solve_rows(): jax.scipy.linalg.solve_triangular(lower, first, lower=True, trans=1)  83.7 us
    psum x1, blocking collectives, shards(): lax.psum(jnp.sum(updated * updated, axis=0), ('dp', 'tensor'))  70.4 us
    another operation x14, matrix products, solve_rows(): lower = jnp.linalg.cholesky(hadamard)  23.3 us
    another operation x24, local copies, waits for them, and re-layouts  22.3 us
  transfers between devices with their start and end apart: 3, of which 2 were waited for; matrix products, arithmetic and copies ran while one was open for 39% of the time, Pallas kernels for 0%

profile of v1, /device:TPU:1, one launch (start us, length us, event | category | flops | bytes accessed | tf_op | source)
XLA Modules:
  0.0 847.3 jit_solution(7015857367234878528)
XLA Ops:
  6.5 2.3 stack.2
  8.8 11.5 %all-to-all-start = ((bf16[128,8,1024]{2,1,0:T(8,128)(2,1)}), bf16[128,8,1024]{2,1,0:T(8,128)(2,1)S(1)}, u32[]{:S(2)}, u32[]{:S(2)}) async-start(bf16[128,8,1024]{2,1,0:T(8,128)(2,1)} %stack.2), calls=%async_computation | async-start | bytes 4194304 | tf_op jit(solution)/shard_map/all_to_all | solution.py:25
  20.4 13.8 %convolution_convert_fusion = bf16[2048,1024]{1,0:T(8,128)(2,1)} fusion(bf16[2048,2048]{1,0:T(8,128)(2,1)} %param.3, bf16[2048,1024]{1,0:T(8,128)(2,1)} %param.4), kind=kOutput, calls=%fused_computation.9 | convolution fusion | flops 8592031744 | bytes 16777216 | tf_op jit(solution)/shard_map/dot_general | solution.py:19
  34.2 17.0 %all-to-all-done = bf16[128,8,1024]{2,1,0:T(8,128)(2,1)S(1)} async-done(((bf16[128,8,1024]{2,1,0:T(8,128)(2,1)}), bf16[128,8,1024]{2,1,0:T(8,128)(2,1)S(1)}, u32[]{:S(2)}, u32[]{:S(2)}) %all-to-all-start) | async-done | bytes 2097184 | tf_op jit(solution)/shard_map/all_to_all | solution.py:25
  51.3 2.4 fusion.102
  53.7 2.0 copy-done
  55.6 2.4 fusion
  58.0 5.8 copy.11
  63.9 4.5 add_multiply_fusion
  68.4 2.0 copy-done.1
  70.4 11.7 %cholesky.222 = f32[128,128]{1,0:T(8,128)S(1)} custom-call(f32[128,128]{1,0:T(8,128)S(1)} %cholesky.577), custom_call_target="Cholesky" | custom-call | tf_op jit(solution)/shard_map/jit(cholesky)/cholesky | solution.py:11
  82.1 2.5 cholesky.254
  84.6 9.8 %custom-call.66 = f32[1,128,128]{1,2,0:T(8,128)S(1)} custom-call(f32[1,128,128]{2,1,0:T(8,128)S(1)} %get-tuple-element.44), custom_call_target="InvertDiagBlocksLowerTriangular" | custom-call | tf_op jit(solution)/shard_map/jit(cholesky)/cholesky | solution.py:11
  94.4 2.3 constant_dynamic-update-slice_fusion.50
  96.8 1.5 convolution_subtract_fusion
  98.3 11.9 %cholesky.243 = f32[128,128]{1,0:T(8,128)S(1)} custom-call(f32[128,128]{1,0:T(8,128)S(1)} %cholesky.581), custom_call_target="Cholesky" | custom-call | tf_op jit(solution)/shard_map/jit(cholesky)/cholesky | solution.py:11
  110.2 5.9 fusion.7
  116.8 9.8 %custom-call.67 = f32[1,128,128]{1,2,0:T(8,128)S(1)} custom-call(f32[1,128,128]{2,1,0:T(8,128)S(1)} %get-tuple-element.41), custom_call_target="InvertDiagBlocksLowerTriangular" | custom-call | tf_op jit(solution)/shard_map/jit(cholesky)/cholesky | solution.py:11
  126.6 1.2 convolution_dynamic-update-slice_fusion
  127.8 2.1 convolution_subtract_fusion.1
  130.0 11.7 %cholesky.466 = f32[128,128]{1,0:T(8,128)S(1)} custom-call(f32[128,128]{1,0:T(8,128)S(1)} %cholesky.586), custom_call_target="Cholesky" | custom-call | tf_op jit(solution)/shard_map/jit(cholesky)/cholesky | solution.py:11
  142.3 9.8 %custom-call.68 = f32[1,128,128]{1,2,0:T(8,128)S(1)} custom-call(f32[1,128,128]{2,1,0:T(8,128)S(1)} %get-tuple-element.38), custom_call_target="InvertDiagBlocksLowerTriangular" | custom-call | tf_op jit(solution)/shard_map/jit(cholesky)/cholesky | solution.py:11
  152.1 1.2 convolution_dynamic-update-slice_fusion.1
  153.3 2.5 convolution_subtract_fusion.2
  155.9 11.7 %cholesky.485 = f32[128,128]{1,0:T(8,128)S(1)} custom-call(f32[128,128]{1,0:T(8,128)S(1)} %cholesky.591), custom_call_target="Cholesky" | custom-call | tf_op jit(solution)/shard_map/jit(cholesky)/cholesky | solution.py:11
  168.2 9.8 %custom-call.69 = f32[1,128,128]{1,2,0:T(8,128)S(1)} custom-call(f32[1,128,128]{2,1,0:T(8,128)S(1)} %get-tuple-element.35), custom_call_target="InvertDiagBlocksLowerTriangular" | custom-call | tf_op jit(solution)/shard_map/jit(cholesky)/cholesky | solution.py:11
  178.0 1.1 convolution_dynamic-update-slice_fusion.2
  179.1 2.4 convolution_subtract_fusion.3
  181.5 11.7 %cholesky.504 = f32[128,128]{1,0:T(8,128)S(1)} custom-call(f32[128,128]{1,0:T(8,128)S(1)} %cholesky.596), custom_call_target="Cholesky" | custom-call | tf_op jit(solution)/shard_map/jit(cholesky)/cholesky | solution.py:11
  193.9 10.1 %custom-call.70 = f32[1,128,128]{1,2,0:T(8,128)S(1)} custom-call(f32[1,128,128]{2,1,0:T(8,128)S(1)} %get-tuple-element.32), custom_call_target="InvertDiagBlocksLowerTriangular" | custom-call | tf_op jit(solution)/shard_map/jit(cholesky)/cholesky | solution.py:11
  205.0 2.3 convolution_subtract_fusion.4
  207.3 11.7 %cholesky.524 = f32[128,128]{1,0:T(8,128)S(1)} custom-call(f32[128,128]{1,0:T(8,128)S(1)} %cholesky.601), custom_call_target="Cholesky" | custom-call | tf_op jit(solution)/shard_map/jit(cholesky)/cholesky | solution.py:11
  219.7 9.8 %custom-call.71 = f32[1,128,128]{1,2,0:T(8,128)S(1)} custom-call(f32[1,128,128]{2,1,0:T(8,128)S(1)} %get-tuple-element.29), custom_call_target="InvertDiagBlocksLowerTriangular" | custom-call | tf_op jit(solution)/shard_map/jit(cholesky)/cholesky | solution.py:11
  230.4 2.0 convolution_subtract_fusion.5
  232.5 11.9 %cholesky.544 = f32[128,128]{1,0:T(8,128)S(1)} custom-call(f32[128,128]{1,0:T(8,128)S(1)} %cholesky.606), custom_call_target="Cholesky" | custom-call | tf_op jit(solution)/shard_map/jit(cholesky)/cholesky | solution.py:11
  245.0 9.8 %custom-call.72 = f32[1,128,128]{1,2,0:T(8,128)S(1)} custom-call(f32[1,128,128]{2,1,0:T(8,128)S(1)} %get-tuple-element.26), custom_call_target="InvertDiagBlocksLowerTriangular" | custom-call | tf_op jit(solution)/shard_map/jit(cholesky)/cholesky | solution.py:11
  255.7 1.8 convolution_subtract_fusion.6
  257.5 11.7 %cholesky.562 = f32[128,128]{1,0:T(8,128)S(1)} custom-call(f32[128,128]{1,0:T(8,128)S(1)} %convolution_subtract_fusion.6), custom_call_target="Cholesky" | custom-call | tf_op jit(solution)/shard_map/jit(cholesky)/cholesky | solution.py:11
  279.3 4.9 select_select_fusion
  284.2 22.5 %while.1 = (s32[]{:T(128)}, f32[1024,1024]{1,0:T(8,128)}, s32[8,2]{0,1:T(2,128)S(1)}, f32[8,128,128]{2,1,0:T(8,128)S(1)}, s32[]{:T(128)}) while((s32[]{:T(128)}, f32[1024,1024]{1,0:T(8,128)}, s32[8,2]{0,1:T(2,128)S(1)}, f32[8,128,128]{2,1,0:T(8,128)S(1)}, s32[]{:T(128)}) %tuple.56), condition=%wide.while_cond, body=%wide.while_body.sunk | while | flops 2 | bytes 131189 | solution.py:13
  284.8 2.2 bitcast_dynamic-update-slice_fusion.2
  287.6 2.2 bitcast_dynamic-update-slice_fusion.2
  290.4 2.2 bitcast_dynamic-update-slice_fusion.2
  293.3 2.2 bitcast_dynamic-update-slice_fusion.2
  296.1 2.2 bitcast_dynamic-update-slice_fusion.2
  298.9 2.2 bitcast_dynamic-update-slice_fusion.2
  301.7 2.2 bitcast_dynamic-update-slice_fusion.2
  304.5 2.1 bitcast_dynamic-update-slice_fusion.2
  306.7 78.8 %custom-call.73 = f32[8,128,128]{1,2,0:T(8,128)S(1)} custom-call(f32[8,128,128]{2,1,0:T(8,128)S(1)} %get-tuple-element.12), custom_call_target="InvertDiagBlocksLowerTriangular" | custom-call | tf_op jit(solution)/shard_map/jit(_solve_triangular)/triangular_solve | solution.py:13
  385.5 362.2 %reduce-scatter.5.cloned.1.call-done = f32[8,1024]{1,0:T(8,128)} async-done(((f32[1024,1024]{1,0:T(8,128)}), f32[8,1024]{1,0:T(8,128)}) %reduce-scatter.5.cloned.1.call-update) | async-done | bytes 32784 | tf_op jit(solution)/shard_map/reduce_scatter | solution.py:29
  749.7 1.1 convolution_subtract_fusion.15
  751.0 1.2 convolution_subtract_fusion.14
  752.4 1.2 convolution_subtract_fusion.13
  753.9 1.4 convolution_subtract_fusion.12
  755.4 1.4 convolution_subtract_fusion.20
  757.0 1.5 convolution_subtract_fusion.19
  759.0 1.0 convolution_subtract_fusion.11
  760.2 1.1 convolution_subtract_fusion.10
  761.5 1.2 convolution_subtract_fusion.9
  762.9 1.2 convolution_subtract_fusion.8
  764.4 1.3 convolution_subtract_fusion.7
  765.9 1.3 convolution_subtract_fusion.18
  767.5 1.4 convolution_subtract_fusion.17
  769.2 70.4 %psum.7 = f32[1024]{0:T(1024)S(1)} all-reduce(f32[1024]{0:T(1024)S(1)} %multiply_reduce_fusion), channel_id=1, replica_groups=mesh['dp'=32,'tensor'=4] {'dp','tensor'}, use_global_device_ids=true, to_apply=%region_19.20 | all-reduce | flops 1024 | bytes 8192 | tf_op jit(solution)/shard_map/psum | solution.py:40
  (93 shorter events, 22.5 us)
Async XLA Ops:
  8.8 42.4 %all-to-all-start = ((bf16[128,8,1024]{2,1,0:T(8,128)(2,1)}), bf16[128,8,1024]{2,1,0:T(8,128)(2,1)S(1)}, u32[]{:S(2)}, u32[]{:S(2)}) async-start(bf16[128,8,1024]{2,1,0:T(8,128)(2,1)} %stack.2), calls=%async_computation | async-start | bytes 4194304 | tf_op jit(solution)/shard_map/all_to_all | solution.py:25
  20.3 89.9 %reduce-scatter.3.cloned.1.call-start = ((), (), s32[]{:S(2)}) async-start(), calls=%async_computation.3 | async-start | bytes 5242880 | tf_op jit(solution)/shard_map/reduce_scatter | solution.py:18
  34.2 713.5 %reduce-scatter.5.cloned.1.call-start = ((), (), s32[]{:S(2)}) async-start(), calls=%async_computation.4 | async-start | bytes 4227072 | tf_op jit(solution)/shard_map/reduce_scatter | solution.py:29
  53.6 2.0 copy-start
  68.4 2.0 copy-start.1
Sparse Core Ops, SparseCore 0:
  34.3 49.8 reduce-scatter.2
  116.2 631.3 reduce-scatter.4
